TPU v7x, 32 devices: a whole 2x2x4 slice. The times are simulated.
32 devices in a mesh: group: 2 (over x), cand: 16 (over z, y, core).
Axes of the slice: x: 2, y: 2, z: 4, core: 2. Of those that a mesh axis runs over, the one named last changes fastest.
Arguments:
- embeddings: bfloat16 [64, 1024, 768], P(('group', 'cand')), parts along dimension 0
- lengths: int32 [64], P(('group', 'cand')), parts along dimension 0, may hold values from 256 to 1024, as said below
Outputs:
- consensus: float32 [64, 1024], P(('group', 'cand')), parts along dimension 0
There are 2 independent parts, one for each index of `group`. A program takes and returns all parts, laid end to end along the dimension named above; each array names one. Nothing has to cross between parts.
Inputs may be any that keep to these rules, and one draw needn't show every extreme that they name: `lengths`: at least one answer of every prompt has exactly 1024 tokens; every answer has 256 tokens or more.
All inputs are finite; a program needn't handle non-finite values.
Results may differ from a plain program's by a relative error of at most 0.0005.
Values may be sent and summed in bfloat16 or wider, within the bound.
A program may use at most 64 MiB of HBM per device.

v0:
```python
import functools

import jax
import jax.numpy as jnp
from jax import lax
from jax.experimental import pallas as pl
from jax.experimental.pallas import tpu as pltpu
from jax.sharding import PartitionSpec as P

MESH = pl.DeviceIdType.MESH
INV_TEMP = 256.0
LOW = -1e30
ROWS = 128
WIDE = 256


def unit_rows(raw):
    values = raw.astype(jnp.float32)
    scale = lax.rsqrt(jnp.sum(values * values, axis=-1, keepdims=True) + 1e-06)
    return (values * scale).astype(jnp.bfloat16)


def kernel(
    n, x_hbm, lens_ref, out_ref,
    raw, units, across, fresh, board, lens, bias, peak, mass, total, back,
    local_sem, send_sem, recv_sem,
):
    answers, length = x_hbm.shape[0], x_hbm.shape[1]
    chunks = length // ROWS
    pieces = answers * chunks
    me = lax.axis_index("cand")
    parity = lax.rem(me, 2)
    partner = me + 1 - 2 * parity
    other = lax.rem(me + n - 1 + 2 * parity, n)

    for a in range(answers):
        lens[0, a : a + 1] = jnp.full((1, 128), lens_ref[a], jnp.int32)

    barrier = pltpu.get_barrier_semaphore()
    for device in (partner, other):
        pl.semaphore_signal(barrier, inc=1, device_id={"cand": device}, device_id_type=MESH)
    local = pltpu.make_async_copy(x_hbm, raw.at[0], local_sem)
    local.start()
    pl.semaphore_wait(barrier, 2)

    def remote(src, dst, sem, device):
        return pltpu.make_async_remote_copy(
            src_ref=src, dst_ref=dst, send_sem=send_sem.at[sem], recv_sem=recv_sem.at[sem],
            device_id={"cand": device}, device_id_type=MESH,
        )

    def piece(i):
        b, k = lax.rem(i, answers), i // answers
        rows = pl.ds(pl.multiple_of(k * ROWS, ROWS), ROWS)
        return remote(x_hbm.at[b, rows], raw.at[2, b, rows], i, other)

    lens_c = remote(lens.at[0], lens.at[1], pieces, partner)
    lens_r = remote(lens.at[0], lens.at[2], pieces + 1, other)
    block_c = remote(x_hbm, raw.at[1], pieces + 2, partner)
    lens_r.start()
    lens_c.start()
    block_c.start()

    def launch(i, carry):
        piece(i).start()
        return carry

    lax.fori_loop(0, pieces, launch, 0)

    lane = lax.broadcasted_iota(jnp.int32, (1, length), 1)
    eye = lax.broadcasted_iota(jnp.int32, (ROWS, ROWS), 0) == lax.broadcasted_iota(
        jnp.int32, (ROWS, ROWS), 1
    )
    total[...] = jnp.zeros_like(total)
    peak[...] = jnp.full_like(peak, LOW)
    mass[...] = jnp.zeros_like(mass)

    def set_bias(slot, counts):
        for a in range(answers):
            bias[slot * answers + a] = jnp.where(lane < counts[a : a + 1, 0:1], 0.0, LOW)

    def normalise(slot):
        def one(i, carry):
            a, k = i // chunks, lax.rem(i, chunks)
            rows = pl.ds(pl.multiple_of(k * ROWS, ROWS), ROWS)
            unit = unit_rows(raw[slot, a, rows])
            units[slot * answers + a, rows] = unit
            across[slot * answers + a, :, rows] = unit.T
            return carry

        lax.fori_loop(0, answers * chunks, one, 0)

    def score(query, left, place):
        for j in range(0, length, WIDE):
            board[pl.ds(place, query.shape[0]), j : j + WIDE] = INV_TEMP * lax.dot_general(
                query, across[left, :, j : j + WIDE], (((1,), (0,)), ((), ())),
                preferred_element_type=jnp.float32,
            ) + bias[left, :, j : j + WIDE]

    def fold(tiles, row_slot, k):
        cols = pl.ds(pl.multiple_of(k * ROWS, ROWS), ROWS)
        row_bias = jnp.broadcast_to(bias[row_slot, :, cols], (ROWS, ROWS))
        row_bias = jnp.sum(jnp.where(eye, row_bias, 0.0), axis=1, keepdims=True)
        term = sum(soften(place, row_bias, pair) for place, pair in tiles)
        term = jnp.sum(jnp.where(eye, jnp.broadcast_to(term, (ROWS, ROWS)), 0.0), axis=0, keepdims=True)
        total[row_slot, :, cols] = total[row_slot, :, cols] + term

    def soften(place, row_bias, pair):
        rows = pl.ds(place, ROWS)
        tops = None
        for j in range(0, length, WIDE):
            scores = board[rows, j : j + WIDE] + row_bias
            board[rows, j : j + WIDE] = scores
            before = peak[pair, :, j : j + WIDE]
            now = jnp.maximum(before, jnp.max(scores, axis=0, keepdims=True))
            peak[pair, :, j : j + WIDE] = now
            mass[pair, :, j : j + WIDE] = mass[pair, :, j : j + WIDE] * jnp.exp(
                before - now
            ) + jnp.sum(jnp.exp(scores - now), axis=0, keepdims=True)
            for i in range(0, WIDE, 128):
                part = scores[:, i : i + 128]
                tops = part if tops is None else jnp.maximum(tops, part)
        top = jnp.max(tops, axis=1, keepdims=True)
        sums = None
        for j in range(0, length, 128):
            part = jnp.exp(board[rows, j : j + 128] - top)
            sums = part if sums is None else sums + part
        return (top + jnp.log(jnp.sum(sums, axis=1, keepdims=True))) / INV_TEMP

    def close(left, pair):
        total[left] = total[left] + (peak[pair] + jnp.log(mass[pair])) / INV_TEMP

    local.wait()
    set_bias(0, lens[0])
    normalise(0)

    def own(k, carry):
        rows = pl.ds(pl.multiple_of(k * (2 * ROWS), 2 * ROWS), 2 * ROWS)
        score(units[1, rows], 0, 0)
        for h in range(2):
            fold([(h * ROWS, 0)], 1, 2 * k + h)
        return carry

    lax.fori_loop(0, chunks // 2, own, 0)
    close(0, 0)

    lens_c.wait()
    block_c.wait()
    set_bias(1, lens[1])
    normalise(1)

    def near(k, carry):
        rows = pl.ds(pl.multiple_of(k * (2 * ROWS), 2 * ROWS), 2 * ROWS)
        for a in range(answers):
            slot = answers + lax.rem(a + parity, 2)
            score(units[slot, rows], a, a * 2 * ROWS)
        for a in range(answers):
            slot = answers + lax.rem(a + parity, 2)
            for h in range(2):
                fold([((2 * a + h) * ROWS, 1 + a)], slot, 2 * k + h)
        return carry

    lax.fori_loop(0, chunks // 2, near, 0)
    for a in range(answers):
        close(a, 1 + a)

    lens_r.wait()
    set_bias(2, lens[2])
    first = 1 + answers

    def far(i, carry):
        piece(i).wait()
        k, b = i // answers, lax.rem(i, answers)
        rows = pl.ds(pl.multiple_of(k * ROWS, ROWS), ROWS)
        fresh[...] = unit_rows(raw[2, b, rows])
        mine = lax.rem(b + parity, answers)
        for a in range(answers):
            score(fresh[...], answers + a, a * ROWS)
        score(fresh[...], mine, answers * ROWS)
        tiles = [(a * ROWS, first + a * answers + b) for a in range(answers)]
        tiles.append((answers * ROWS, first + answers * answers + mine))
        fold(tiles, 2 * answers + b, k)
        return carry

    lax.fori_loop(0, answers * chunks, far, 0)

    back_r = remote(total.at[pl.ds(2 * answers, answers)], back.at[1], pieces + 3, other)
    back_c = remote(total.at[pl.ds(answers, answers)], back.at[0], pieces + 4, partner)
    for p in range(answers * answers):
        close(answers + p // answers, first + p)
    back_r.start()
    for a in range(answers):
        close(a, first + answers * answers + a)
    back_c.start()
    back_c.wait()
    back_r.wait()
    for a in range(answers):
        whole = total[a] + back[0, a] + back[1, a]
        out_ref[a : a + 1] = jnp.where(bias[a] == 0.0, whole, 0.0)


def solution(mesh):
    n = mesh.shape["cand"]

    def shards(embeddings, lengths):
        answers, length, width = embeddings.shape
        chunks = length // ROWS
        pairs = 1 + 2 * answers + answers * answers
        sums = pl.pallas_call(
            functools.partial(kernel, n),
            out_shape=jax.ShapeDtypeStruct((answers, length), jnp.float32),
            in_specs=[
                pl.BlockSpec(memory_space=pl.ANY),
                pl.BlockSpec(memory_space=pltpu.SMEM),
            ],
            out_specs=pl.BlockSpec(memory_space=pltpu.VMEM),
            scratch_shapes=[
                pltpu.VMEM((3, answers, length, width), jnp.bfloat16),
                pltpu.VMEM((2 * answers, length, width), jnp.bfloat16),
                pltpu.VMEM((2 * answers, width, length), jnp.bfloat16),
                pltpu.VMEM((ROWS, width), jnp.bfloat16),
                pltpu.VMEM((2 * answers * ROWS, length), jnp.float32),
                pltpu.VMEM((3, answers, 128), jnp.int32),
                pltpu.VMEM((3 * answers, 1, length), jnp.float32),
                pltpu.VMEM((pairs, 1, length), jnp.float32),
                pltpu.VMEM((pairs, 1, length), jnp.float32),
                pltpu.VMEM((3 * answers, 1, length), jnp.float32),
                pltpu.VMEM((2, answers, 1, length), jnp.float32),
                pltpu.SemaphoreType.DMA,
                pltpu.SemaphoreType.DMA((answers * chunks + 5,)),
                pltpu.SemaphoreType.DMA((answers * chunks + 5,)),
            ],
            compiler_params=pltpu.CompilerParams(collective_id=0, has_side_effects=True),
            name="consensus",
        )(embeddings, lengths)
        return sums / (answers - 1 + 4 * answers)

    return jax.shard_map(
        shards,
        mesh=mesh,
        in_specs=(P(("group", "cand"), None, None), P(("group", "cand"))),
        out_specs=P(("group", "cand"), None),
        check_vma=False,
    )
```

profile of v0, /device:TPU:1, one launch (start us, length us, event | category | flops | bytes accessed | tf_op | source)
XLA Modules:
  0.0 79.0 jit_solution(3009691939001798421)
XLA Ops:
  0.0 77.7 %consensus.1 = f32[2,1024]{1,0:T(2,128)} custom-call(bf16[2,1024,768]{2,1,0:T(8,128)(2,1)} %x_hbm.1, s32[2]{0:T(128)} %lens_ref.1), custom_call_target="tpu_custom_call" | custom-call | tf_op jit(solution)/shard_map/consensus/pallas_call | solution.py:209
  77.7 1.3 %broadcast_multiply_fusion = f32[2,1024]{1,0:T(2,128)} fusion(f32[2,1024]{1,0:T(2,128)} %consensus.1), kind=kLoop, calls=%fused_computation | loop fusion | flops 2048 | bytes 16384 | tf_op jit(solution)/shard_map/div | solution.py:236
where the time goes:
time: 79.2 us; the launch traced here: 79 us
  Pallas kernels  77.7 us (98%)
  other arithmetic  1.3 us (2%)
    pallas_call x1, Pallas kernels, shards(): pl.pallas_call(functools.partial(kernel, n), out_shape=jax.ShapeDtypeStru...  77.7 us

commit v1 on v0

v1 whole, which is shorter than its diff:
```python
import functools
import math

import jax
import jax.numpy as jnp
from jax import lax
from jax.experimental import pallas as pl
from jax.experimental.pallas import tpu as pltpu
from jax.sharding import PartitionSpec as P

MESH = pl.DeviceIdType.MESH
SCALE = 256.0 * math.log2(math.e)
LOW = -1e30
PIECE = 128
ROWS = 256
WIDE = 256
DETOUR = (3, 3)
RING = (-4, -3, -2, -1, 1, 2, 3, 4)
LENS = (-3, -2, -1, 1, 2)


def unit_rows(raw):
    values = raw.astype(jnp.float32)
    scale = lax.rsqrt(jnp.sum(values * values, axis=-1, keepdims=True) + 1e-06)
    return (values * scale).astype(jnp.bfloat16)


def kernel(
    n, detour, x_hbm, lens_ref, out_ref,
    raw, units, far, relay, fresh, board_a, board_b, lens, bias, peak, mass, total, back,
    local_sem, near_sems, lens_send, lens_recv, send_sem, far_recv, pass_send, relay_recv, relay_send,
    back_send, back_recv,
):
    length = x_hbm.shape[1]
    chunks = length // PIECE
    per = ROWS // PIECE
    boards = (board_a, board_b)
    group = lax.axis_index("group")
    place = lax.axis_index("cand")
    twin = group + 1 - 2 * lax.rem(group, 2)
    flip = lax.rem(group, 2)
    me = place + flip * (n - 1 - 2 * place)
    role = lax.rem(me, 4)
    core = lax.rem(me, 2)
    partner = me + 1 - 2 * core
    even, odd = role < 2, role >= 2

    def spot(m):
        m = lax.rem(m + n, n)
        return m + flip * (n - 1 - 2 * m)

    def ring(m):
        return (group, spot(m))

    across = (twin, place)
    corner = (twin, spot(jnp.where(even, me + 2, me - 2)))

    for a in range(2):
        lens[0, a : a + 1] = jnp.full((1, 128), lens_ref[a], jnp.int32)

    barrier = pltpu.get_barrier_semaphore()
    meets = [ring(me + d) for d in RING]
    if sum(detour):
        meets += [across, corner]
    for device in meets:
        pl.semaphore_signal(barrier, inc=1, device_id=device, device_id_type=MESH)
    local = pltpu.make_async_copy(x_hbm, raw.at[0], local_sem)
    local.start()
    pl.semaphore_wait(barrier, len(meets))

    def remote(src, dst, send, recv, device):
        return pltpu.make_async_remote_copy(
            src_ref=src, dst_ref=dst, send_sem=send, recv_sem=recv,
            device_id=device, device_id_type=MESH,
        )

    def rows_of(k):
        return pl.ds(pl.multiple_of(k * PIECE, PIECE), PIECE)

    def spread(i):
        d = LENS[i]
        return remote(lens.at[0], lens.at[1 + i], lens_send.at[i], lens_recv.at[i], ring(me - d))

    near = remote(x_hbm, raw.at[1], near_sems.at[0], near_sems.at[1], ring(partner))

    def own_piece(a, k, slot, device):
        return remote(x_hbm.at[a, rows_of(k)], far.at[slot, rows_of(k)], send_sem.at[a, k], far_recv.at[slot, k], device)

    def around(a, k):
        return remote(x_hbm.at[a, rows_of(k)], relay.at[a, k], send_sem.at[a, k], relay_recv.at[a, k], corner)

    def bypass(a, k):
        return remote(relay.at[a, k], far.at[a, rows_of(k)], relay_send.at[a, k], far_recv.at[a, k], across)

    def detours(a, k):
        return k % 2 == 1 and k // 2 < detour[a]

    order = [(a, k) for k in range(chunks) for a in range(2)]
    for i in range(len(LENS)):
        spread(i).start()

    @pl.when(role == 3)
    def _():
        for a, k in order:
            if detours(a, k):
                around(a, k).start()
        for a, k in order:
            if not detours(a, k):
                own_piece(a, k, a, ring(me - 2)).start()

    @pl.when(role == 2)
    def _():
        for a, k in order:
            own_piece(a, k, a, ring(me - 2)).start()

    @pl.when(role == 0)
    def _():
        for a, k in order:
            own_piece(a, k, 0, ring(me + 2 + a)).start()

    @pl.when(role != 0)
    def _():
        near.start()

    lane = lax.broadcasted_iota(jnp.int32, (1, length), 1)
    row = lax.broadcasted_iota(jnp.int32, (PIECE, 128), 0)
    eye = lax.broadcasted_iota(jnp.int32, (PIECE, PIECE), 0) == lax.broadcasted_iota(
        jnp.int32, (PIECE, PIECE), 1
    )
    total[...] = jnp.zeros_like(total)
    peak[...] = jnp.full_like(peak, LOW)
    mass[...] = jnp.zeros_like(mass)

    def set_bias(slot, counts):
        for a in range(2):
            bias[slot + a] = jnp.where(lane < counts[a : a + 1, 0:1], 0.0, LOW)

    def normalise(slot):
        def one(i, carry):
            a, k = i // chunks, lax.rem(i, chunks)
            units[2 * slot + a, rows_of(k)] = unit_rows(raw[slot, a, rows_of(k)])
            return carry

        lax.fori_loop(0, 2 * chunks, one, 0)

    def unit(query, left, count, halves):
        for a in range(count):
            for j in range(0, length, WIDE):
                boards[a][:, j : j + WIDE] = lax.dot_general(
                    query, units[left + a, j : j + WIDE], (((1,), (1,)), ((), ())),
                    preferred_element_type=jnp.float32,
                )
        for h, (counts, first, pair, slot) in enumerate(halves):
            part = slice(h * PIECE, (h + 1) * PIECE)
            row_bias = jnp.where(row + first < counts, 0.0, LOW)
            term = None
            for a in range(count):
                value = soften(boards[a], part, left + a, pair + a, row_bias)
                term = value if term is None else term + value
            cols = pl.ds(pl.multiple_of(first, PIECE), PIECE)
            total[slot, :, cols] = total[slot, :, cols] + jnp.sum(
                jnp.where(eye, jnp.broadcast_to(term, (PIECE, PIECE)), 0.0), axis=0, keepdims=True
            )

    def soften(board, part, left, pair, row_bias):
        tops = None
        for j in range(0, length, 128):
            cols = slice(j, j + 128)
            scores = board[part, cols] * SCALE + bias[left, :, cols] + row_bias
            board[part, cols] = scores
            tops = scores if tops is None else jnp.maximum(tops, scores)
            before = peak[pair, :, cols]
            now = jnp.maximum(before, jnp.max(scores, axis=0, keepdims=True))
            peak[pair, :, cols] = now
            mass[pair, :, cols] = mass[pair, :, cols] * jnp.exp2(before - now)
        top = jnp.max(tops, axis=1, keepdims=True)
        wide = jnp.broadcast_to(top, (PIECE, 128))
        sums = None
        for j in range(0, length, 128):
            cols = slice(j, j + 128)
            scores = board[part, cols]
            value = jnp.exp2(scores - wide)
            sums = value if sums is None else sums + value
            value = jnp.exp2(scores - peak[pair, :, cols])
            mass[pair, :, cols] = mass[pair, :, cols] + jnp.sum(value, axis=0, keepdims=True)
        return top + jnp.log2(jnp.sum(sums, axis=1, keepdims=True))

    def close(slot, pair):
        total[slot] = total[slot] + peak[pair] + jnp.log2(mass[pair])

    local.wait()
    set_bias(0, lens[0])
    normalise(0)
    for i in range(len(LENS)):
        spread(i).wait()

    @pl.when(role != 1)
    def _():
        near.wait_recv()
        set_bias(2, lens[1 + LENS.index(1)])
        normalise(1)

    @pl.when((role == 1) | (role == 3))
    def _():
        set_bias(2, lens[1 + LENS.index(-1)])

    def lens_at(d, a):
        return lens[1 + LENS.index(d), a : a + 1]

    base = jnp.where((role == 0) | (role == 3), 2, 0)
    last = jnp.where(role >= 2, 2 - base, base)

    def arrive(slot, k):
        remote(x_hbm.at[0, rows_of(k)], far.at[slot, rows_of(k)], pass_send.at[0, 0], far_recv.at[slot, k], across).wait_recv()

    def passing(slot, k):
        target = jnp.where(even, me + 4, me - 4)
        there = jnp.where(even, slot + 2, slot + 1)
        return remote(far.at[slot, rows_of(k)], far.at[there, rows_of(k)], pass_send.at[slot, k], far_recv.at[there, k], ring(target))

    def hand_on(slot, k):
        arrive(slot, k)
        passing(slot, k).start()

    def tile_rows(tile):
        return pl.ds(pl.multiple_of(tile * ROWS, ROWS), ROWS)

    def take_local(slot, k, stage, h):
        fresh[stage, h * PIECE : (h + 1) * PIECE] = units[slot, rows_of(k)]

    def take_far(slot, k, stage, h):
        fresh[stage, h * PIECE : (h + 1) * PIECE] = unit_rows(far[slot, rows_of(k)])

    counts = [None] * 4
    own_len = [lens[0, a : a + 1] for a in range(2)]
    is0, is1, is2, is3 = (jnp.full((1, 128), role, jnp.int32) == r for r in range(4))
    pick = lambda v0, v1, v2, v3: jnp.where(is0, v0, jnp.where(is1, v1, jnp.where(is2, v2, v3)))
    counts[0] = pick(own_len[0], lens_at(2, 0), lens_at(1, 0), own_len[1])
    counts[1] = pick(own_len[1], lens_at(2, 1), lens_at(-2, 0), lens_at(-3, 1))
    counts[2] = pick(lens_at(2, 0), lens_at(-2, 0), lens_at(2, 0), lens_at(1, 1))
    counts[3] = pick(lens_at(2, 1), lens_at(-2, 1), lens_at(2, 0), lens_at(1, 1))
    choose = lambda v0, v1, v2, v3: jnp.where(role == 0, v0, jnp.where(role == 1, v1, jnp.where(role == 2, v2, v3)))
    slots = [choose(0, 4, 2, 1), choose(1, 5, 4, 4), choose(4, 6, 5, 5), choose(5, 7, 5, 5)]

    routed = [(a, k) for a, k in order if detours(a, k)]

    def step(j, carry):
        @pl.when(j < chunks)
        def _():
            @pl.when(role == 1)
            def _():
                hand_on(0, j)
                take_far(0, j, 0, 0)

            @pl.when(role != 1)
            def _():
                take_local(choose(0, 0, 2, 1), j, 0, 0)

            @pl.when(role == 2)
            def _():
                for i, (a, k) in enumerate(routed):
                    @pl.when(j == i * chunks // len(routed))
                    def _():
                        around(a, k).wait_recv()
                        bypass(a, k).start()

            @pl.when(role == 0)
            def _():
                take_local(1, j, 0, 1)

            @pl.when(role != 0)
            def _():
                slot = jnp.where(role == 1, 1, 0)
                hand_on(slot, j)
                take_far(slot, j, 0, 1)

            unit(fresh[0], base, 2, [(counts[0], j * PIECE, 0, slots[0]), (counts[1], j * PIECE, 2, slots[1])])

            @pl.when(lax.rem(j, per) == 0)
            def _():
                unit(units[1, tile_rows(j // per)], 0, 1, [(own_len[1], (j + h) * PIECE, 8, 1) for h in range(per)])

        @pl.when(j >= per)
        def _():
            k = j - per
            late = lax.rem(j, per)

            @pl.when(even)
            def _():
                for h in range(2):
                    slot = choose(h, 2 + h, 0, 0)
                    arrive(slot, k)
                    take_far(slot, k, 1, h)

            @pl.when(odd & (late == 0))
            def _():
                for h in range(per):
                    arrive(1, k + h)
                    take_far(1, k + h, 1, h)

            left = jnp.where(late == 0, base, last)
            unit(
                fresh[1], left, 2,
                [
                    (counts[2], jnp.where(even, k, k - late) * PIECE, jnp.where(even, 4, 4 + 2 * late), slots[2]),
                    (counts[3], jnp.where(even, k, k - late + 1) * PIECE, jnp.where(even, 6, 4 + 2 * late), slots[3]),
                ],
            )

        return carry

    lax.fori_loop(0, chunks + per, step, 0)

    close(0, 8)
    for s in range(4):
        left = last if s == 3 else base
        for a in range(2):
            close(left + a, 2 * s + a)

    def give(src, dst, device):
        return remote(total.at[src], back.at[dst], back_send.at[src], back_recv.at[dst], device)

    gives = (
        [give(2, 0, ring(partner)), give(3, 1, ring(partner)), give(4, 2, ring(me + 2)), give(5, 3, ring(me + 2))],
        [give(4, 2, ring(me + 2)), give(5, 3, ring(me + 2)), give(6, 4, ring(me - 2)), give(7, 5, ring(me - 2))],
        [give(2, 0, ring(partner)), give(3, 1, ring(partner)), give(4, 2, ring(me - 2)), give(5, 4, ring(me + 2))],
        [give(2, 0, ring(partner)), give(3, 1, ring(partner)), give(4, 3, ring(me - 3)), give(5, 5, ring(me + 1))],
    )
    takes = ([2, 3, 4, 5], [0, 1], [0, 1, 2, 3], [0, 1, 2, 3, 4, 5])
    for r in range(4):
        @pl.when(role == r)
        def _():
            for copy in gives[r]:
                copy.start()
            for copy in gives[r]:
                copy.wait_send()
            for b in takes[r]:
                give(0, b, ring(partner)).wait_recv()
            for a in range(2):
                whole = total[a]
                for b in takes[r]:
                    if b % 2 == a:
                        whole = whole + back[b]
                out_ref[a : a + 1] = jnp.where(bias[a] == 0.0, whole, 0.0)

    @pl.when(role != 0)
    def _():
        near.wait_send()

    @pl.when(role != 1)
    def _():
        for a, k in order:
            own_piece(a, k, a, ring(partner)).wait_send()

    @pl.when(role == 1)
    def _():
        for a, k in order:
            passing(a, k).wait_send()

    @pl.when(odd)
    def _():
        for k in range(chunks):
            passing(0, k).wait_send()

    @pl.when(role == 2)
    def _():
        for a, k in routed:
            bypass(a, k).wait_send()


def solution(mesh):
    n = mesh.shape["cand"]
    detour = DETOUR if mesh.shape["group"] % 2 == 0 else (0, 0)

    def shards(embeddings, lengths):
        answers, length, width = embeddings.shape
        chunks = length // PIECE
        dma = pltpu.SemaphoreType.DMA
        sums = pl.pallas_call(
            functools.partial(kernel, n, detour),
            out_shape=jax.ShapeDtypeStruct((answers, length), jnp.float32),
            in_specs=[
                pl.BlockSpec(memory_space=pl.ANY),
                pl.BlockSpec(memory_space=pltpu.SMEM),
            ],
            out_specs=pl.BlockSpec(memory_space=pltpu.VMEM),
            scratch_shapes=[
                pltpu.VMEM((2, answers, length, width), jnp.bfloat16),
                pltpu.VMEM((4, length, width), jnp.bfloat16),
                pltpu.VMEM((4, length, width), jnp.bfloat16),
                pltpu.VMEM((2, chunks, PIECE, width), jnp.bfloat16),
                pltpu.VMEM((2, ROWS, width), jnp.bfloat16),
                pltpu.VMEM((ROWS, length), jnp.float32),
                pltpu.VMEM((ROWS, length), jnp.float32),
                pltpu.VMEM((1 + len(LENS), answers, 128), jnp.int32),
                pltpu.VMEM((4, 1, length), jnp.float32),
                pltpu.VMEM((9, 1, length), jnp.float32),
                pltpu.VMEM((9, 1, length), jnp.float32),
                pltpu.VMEM((8, 1, length), jnp.float32),
                pltpu.VMEM((6, 1, length), jnp.float32),
                dma, dma((2,)), dma((len(LENS),)), dma((len(LENS),)),
                dma((2, chunks)), dma((4, chunks)), dma((2, chunks)),
                dma((2, chunks)), dma((2, chunks)), dma((8,)), dma((6,)),
            ],
            compiler_params=pltpu.CompilerParams(collective_id=0, has_side_effects=True),
            name="consensus",
        )(embeddings, lengths)
        return sums * (math.log(2.0) / (256.0 * (answers - 1 + 4 * answers)))

    return jax.shard_map(
        shards,
        mesh=mesh,
        in_specs=(P(("group", "cand"), None, None), P(("group", "cand"))),
        out_specs=P(("group", "cand"), None),
        check_vma=False,
    )
```

time: 79.2 us -> 77.2 us (0.975)
  the two profiles are of different devices: /device:TPU:1 before, /device:TPU:2 now
where the time goes in v1:
time: 77.2 us; the launch traced here: 77 us
  Pallas kernels  75.7 us (98%)
  other arithmetic  1.3 us (2%)
    pallas_call x1, Pallas kernels, shards(): pl.pallas_call(functools.partial(kernel, n, detour), out_shape=jax.ShapeD...  75.7 us

profile of v1, /device:TPU:2, one launch (start us, length us, event | category | flops | bytes accessed | tf_op | source)
XLA Modules:
  0.0 77.0 jit_solution(2107891952132689273)
XLA Ops:
  0.0 75.7 %consensus.1 = f32[2,1024]{1,0:T(2,128)} custom-call(bf16[2,1024,768]{2,1,0:T(8,128)(2,1)} %x_hbm.1, s32[2]{0:T(128)} %lens_ref.1), custom_call_target="tpu_custom_call" | custom-call | tf_op jit(solution)/shard_map/consensus/pallas_call | solution.py:379
  75.7 1.3 %broadcast_multiply_fusion = f32[2,1024]{1,0:T(2,128)} fusion(f32[2,1024]{1,0:T(2,128)} %consensus.1), kind=kLoop, calls=%fused_computation | loop fusion | flops 2048 | bytes 16384 | tf_op jit(solution)/shard_map/mul | solution.py:408

commit v2 on v1

--- a/solution.py
+++ b/solution.py
@@ -15,8 +15,8 @@
 ROWS = 256
 WIDE = 256
 DETOUR = (3, 3)
-RING = (-4, -3, -2, -1, 1, 2, 3, 4)
-LENS = (-3, -2, -1, 1, 2)
+PACE = (0, 2, 2, 2, 0, 0, 0, 0)
+TURN = 1
 
 
 def unit_rows(raw):
@@ -28,8 +28,8 @@
 def kernel(
     n, detour, x_hbm, lens_ref, out_ref,
     raw, units, far, relay, fresh, board_a, board_b, lens, bias, peak, mass, total, back,
-    local_sem, near_sems, lens_send, lens_recv, send_sem, far_recv, pass_send, relay_recv, relay_send,
-    back_send, back_recv,
+    local_sem, near_sems, lens_send, lens_recv, send_sem, far_recv, pass_send, turn_send, relay_recv, relay_send,
+    back_send, back_recv, up_sem, down_sem,
 ):
     length = x_hbm.shape[1]
     chunks = length // PIECE
@@ -59,14 +59,41 @@
         lens[0, a : a + 1] = jnp.full((1, 128), lens_ref[a], jnp.int32)
 
     barrier = pltpu.get_barrier_semaphore()
-    meets = [ring(me + d) for d in RING]
-    if sum(detour):
-        meets += [across, corner]
+    quad, quads = me // 4, n // 4
+    below, above = quad > 0, quad < quads - 1
+    meets = [ring(me - role + lax.rem(role + i, 4)) for i in range(1, 4)] + [across, corner]
     for device in meets:
         pl.semaphore_signal(barrier, inc=1, device_id=device, device_id_type=MESH)
+
+    @pl.when(below)
+    def _():
+        pl.semaphore_signal(barrier, inc=1, device_id=ring(me - 4), device_id_type=MESH)
+
+    @pl.when(above)
+    def _():
+        pl.semaphore_signal(barrier, inc=1, device_id=ring(me + 4), device_id_type=MESH)
+
     local = pltpu.make_async_copy(x_hbm, raw.at[0], local_sem)
     local.start()
-    pl.semaphore_wait(barrier, len(meets))
+    pl.semaphore_wait(barrier, len(meets) + below.astype(jnp.int32) + above.astype(jnp.int32))
+
+    def rise():
+        @pl.when(below)
+        def _():
+            pl.semaphore_wait(up_sem, 1)
+
+        @pl.when(above)
+        def _():
+            pl.semaphore_signal(up_sem, inc=1, device_id=ring(me + 4), device_id_type=MESH)
+
+    def fall():
+        @pl.when(above)
+        def _():
+            pl.semaphore_wait(down_sem, 1)
+
+        @pl.when(below)
+        def _():
+            pl.semaphore_signal(down_sem, inc=1, device_id=ring(me - 4), device_id_type=MESH)
 
     def remote(src, dst, send, recv, device):
         return pltpu.make_async_remote_copy(
@@ -77,51 +104,82 @@
     def rows_of(k):
         return pl.ds(pl.multiple_of(k * PIECE, PIECE), PIECE)
 
-    def spread(i):
-        d = LENS[i]
-        return remote(lens.at[0], lens.at[1 + i], lens_send.at[i], lens_recv.at[i], ring(me - d))
+    def spread(i, slot, device):
+        return remote(lens.at[0], lens.at[slot], lens_send.at[i], lens_recv.at[slot], device)
+
+    def further():
+        target = jnp.where(even, me + 4, me - 4)
+        return remote(lens.at[2], lens.at[3], lens_send.at[3], lens_recv.at[3], ring(target))
+
+    def meet_far():
+        @pl.when(2 * quad < quads)
+        def _():
+            rise()
+            fall()
+
+        @pl.when(2 * quad >= quads)
+        def _():
+            fall()
+            rise()
 
     near = remote(x_hbm, raw.at[1], near_sems.at[0], near_sems.at[1], ring(partner))
 
-    def own_piece(a, k, slot, device):
-        return remote(x_hbm.at[a, rows_of(k)], far.at[slot, rows_of(k)], send_sem.at[a, k], far_recv.at[slot, k], device)
+    def piece(src, a, k, slot, device):
+        return remote(src.at[a, rows_of(k)], far.at[slot, rows_of(k)], send_sem.at[a, k], far_recv.at[slot, k], device)
 
     def around(a, k):
-        return remote(x_hbm.at[a, rows_of(k)], relay.at[a, k], send_sem.at[a, k], relay_recv.at[a, k], corner)
+        return remote(x_hbm.at[a, rows_of(k)], relay.at[a, k], turn_send.at[a, k], relay_recv.at[a, k], corner)
 
     def bypass(a, k):
         return remote(relay.at[a, k], far.at[a, rows_of(k)], relay_send.at[a, k], far_recv.at[a, k], across)
 
-    def detours(a, k):
-        return k % 2 == 1 and k // 2 < detour[a]
-
-    order = [(a, k) for k in range(chunks) for a in range(2)]
-    for i in range(len(LENS)):
-        spread(i).start()
+    routed = [(a, k) for k in range(chunks) for a in range(2) if k < detour[a]]
+    starts = [min(sum(PACE[:i]), len(routed)) for i in range(len(PACE))] + [len(routed)]
+    direct = [[k for k in range(chunks) if (a, k) not in routed] for a in range(2)]
+
+    spread(0, 1, ring(partner)).start()
+
+    @pl.when(odd)
+    def _():
+        spread(1, 2, ring(me - 2)).start()
+
+    @pl.when(role == 0)
+    def _():
+        spread(1, 2, ring(me + 2)).start()
+        spread(2, 2, ring(me + 3)).start()
+
+    @pl.when(role != 0)
+    def _():
+        near.start()
+
+    @pl.when(role == 0)
+    def _():
+        for k in range(chunks):
+            for a in range(2):
+                piece(x_hbm, a, k, 0, ring(me + 2 + a)).start()
 
     @pl.when(role == 3)
     def _():
-        for a, k in order:
-            if detours(a, k):
-                around(a, k).start()
-        for a, k in order:
-            if not detours(a, k):
-                own_piece(a, k, a, ring(me - 2)).start()
+        for k in range(chunks):
+            piece(x_hbm, 0, k, 0, ring(me - 2)).start()
+
+    @pl.when(odd)
+    def _():
+        near.wait_recv()
 
     @pl.when(role == 2)
     def _():
-        for a, k in order:
-            own_piece(a, k, a, ring(me - 2)).start()
-
-    @pl.when(role == 0)
-    def _():
-        for a, k in order:
-            own_piece(a, k, 0, ring(me + 2 + a)).start()
-
-    @pl.when(role != 0)
-    def _():
-        near.start()
-
+        for k in range(chunks):
+            piece(raw.at[1], 1, k, 1, ring(me - 1)).start()
+        for k in direct[0]:
+            piece(x_hbm, 0, k, 0, ring(me - 2)).start()
+
+    @pl.when(role == 3)
+    def _():
+        for k in direct[1]:
+            piece(raw.at[1], 1, k, 1, ring(me - 3)).start()
+
+    meet_far()
     lane = lax.broadcasted_iota(jnp.int32, (1, length), 1)
     row = lax.broadcasted_iota(jnp.int32, (PIECE, 128), 0)
     eye = lax.broadcasted_iota(jnp.int32, (PIECE, PIECE), 0) == lax.broadcasted_iota(
@@ -191,21 +249,21 @@
     local.wait()
     set_bias(0, lens[0])
     normalise(0)
-    for i in range(len(LENS)):
-        spread(i).wait()
+    spread(0, 1, ring(partner)).wait_recv()
+    spread(1, 2, ring(partner)).wait_recv()
+
+    @pl.when(role != 0)
+    def _():
+        further().start()
+
+    @pl.when(role == 0)
+    def _():
+        near.wait_recv()
 
     @pl.when(role != 1)
     def _():
-        near.wait_recv()
-        set_bias(2, lens[1 + LENS.index(1)])
+        set_bias(2, lens[1])
         normalise(1)
-
-    @pl.when((role == 1) | (role == 3))
-    def _():
-        set_bias(2, lens[1 + LENS.index(-1)])
-
-    def lens_at(d, a):
-        return lens[1 + LENS.index(d), a : a + 1]
 
     base = jnp.where((role == 0) | (role == 3), 2, 0)
     last = jnp.where(role >= 2, 2 - base, base)
@@ -231,20 +289,47 @@
     def take_far(slot, k, stage, h):
         fresh[stage, h * PIECE : (h + 1) * PIECE] = unit_rows(far[slot, rows_of(k)])
 
-    counts = [None] * 4
     own_len = [lens[0, a : a + 1] for a in range(2)]
     is0, is1, is2, is3 = (jnp.full((1, 128), role, jnp.int32) == r for r in range(4))
     pick = lambda v0, v1, v2, v3: jnp.where(is0, v0, jnp.where(is1, v1, jnp.where(is2, v2, v3)))
-    counts[0] = pick(own_len[0], lens_at(2, 0), lens_at(1, 0), own_len[1])
-    counts[1] = pick(own_len[1], lens_at(2, 1), lens_at(-2, 0), lens_at(-3, 1))
-    counts[2] = pick(lens_at(2, 0), lens_at(-2, 0), lens_at(2, 0), lens_at(1, 1))
-    counts[3] = pick(lens_at(2, 1), lens_at(-2, 1), lens_at(2, 0), lens_at(1, 1))
+
+    def lens_at(slot, a):
+        return lens[slot, a : a + 1]
+
+    def soon():
+        return (
+            pick(own_len[0], lens_at(2, 0), lens_at(1, 0), own_len[1]),
+            pick(own_len[1], lens_at(2, 1), lens_at(2, 0), lens_at(2, 1)),
+        )
+
+    def later():
+        return (
+            pick(lens_at(2, 0), lens_at(3, 0), lens_at(3, 0), lens_at(3, 1)),
+            pick(lens_at(2, 1), lens_at(3, 1), lens_at(3, 0), lens_at(3, 1)),
+        )
+
     choose = lambda v0, v1, v2, v3: jnp.where(role == 0, v0, jnp.where(role == 1, v1, jnp.where(role == 2, v2, v3)))
     slots = [choose(0, 4, 2, 1), choose(1, 5, 4, 4), choose(4, 6, 5, 5), choose(5, 7, 5, 5)]
 
-    routed = [(a, k) for a, k in order if detours(a, k)]
+    def routes(j, act):
+        for i in range(len(PACE)):
+            if starts[i] < starts[i + 1]:
+                @pl.when(j == i)
+                def _():
+                    for a, k in routed[starts[i] : starts[i + 1]]:
+                        act(a, k)
+
+    def turn(a, k):
+        around(a, k).wait_recv()
+        bypass(a, k).start()
+
+    lag = jnp.where(role == 0, chunks, per)
 
     def step(j, carry):
+        @pl.when(role == 2)
+        def _():
+            routes(j, lambda a, k: around(a, k).start())
+
         @pl.when(j < chunks)
         def _():
             @pl.when(role == 1)
@@ -255,14 +340,6 @@
             @pl.when(role != 1)
             def _():
                 take_local(choose(0, 0, 2, 1), j, 0, 0)
-
-            @pl.when(role == 2)
-            def _():
-                for i, (a, k) in enumerate(routed):
-                    @pl.when(j == i * chunks // len(routed))
-                    def _():
-                        around(a, k).wait_recv()
-                        bypass(a, k).start()
 
             @pl.when(role == 0)
             def _():
@@ -274,16 +351,22 @@
                 hand_on(slot, j)
                 take_far(slot, j, 0, 1)
 
+            counts = soon()
             unit(fresh[0], base, 2, [(counts[0], j * PIECE, 0, slots[0]), (counts[1], j * PIECE, 2, slots[1])])
 
             @pl.when(lax.rem(j, per) == 0)
             def _():
                 unit(units[1, tile_rows(j // per)], 0, 1, [(own_len[1], (j + h) * PIECE, 8, 1) for h in range(per)])
 
-        @pl.when(j >= per)
-        def _():
-            k = j - per
-            late = lax.rem(j, per)
+        @pl.when((j >= lag) & (j < lag + chunks))
+        def _():
+            k = j - lag
+            late = lax.rem(k, per)
+
+            @pl.when((j == lag) & (role != 0))
+            def _():
+                further().wait_recv()
+
 
             @pl.when(even)
             def _():
@@ -299,17 +382,37 @@
                     take_far(1, k + h, 1, h)
 
             left = jnp.where(late == 0, base, last)
+            counts = later()
             unit(
                 fresh[1], left, 2,
                 [
-                    (counts[2], jnp.where(even, k, k - late) * PIECE, jnp.where(even, 4, 4 + 2 * late), slots[2]),
-                    (counts[3], jnp.where(even, k, k - late + 1) * PIECE, jnp.where(even, 6, 4 + 2 * late), slots[3]),
+                    (counts[0], jnp.where(even, k, k - late) * PIECE, jnp.where(even, 4, 4 + 2 * late), slots[2]),
+                    (counts[1], jnp.where(even, k, k - late + 1) * PIECE, jnp.where(even, 6, 4 + 2 * late), slots[3]),
                 ],
             )
 
+        @pl.when(role == 3)
+        def _():
+            routes(j - TURN, turn)
+
         return carry
 
-    lax.fori_loop(0, chunks + per, step, 0)
+    lax.fori_loop(0, 2 * chunks, step, 0)
+
+    def give(src, dst, device):
+        return remote(total.at[src], back.at[dst], back_send.at[src], back_recv.at[dst], device)
+
+    gives = (
+        [give(4, 2, ring(me + 2)), give(5, 3, ring(me + 2))],
+        [give(6, 4, ring(me - 2)), give(7, 5, ring(me - 2)), give(4, 2, ring(me + 2)), give(5, 3, ring(me + 2))],
+        [give(5, 4, ring(me + 2)), give(4, 2, ring(me - 2))],
+        [give(5, 5, ring(me + 1)), give(4, 3, ring(me - 3))],
+    )
+    for r in range(4):
+        @pl.when(role == r)
+        def _():
+            for copy in gives[r]:
+                copy.start()
 
     close(0, 8)
     for s in range(4):
@@ -317,23 +420,15 @@
         for a in range(2):
             close(left + a, 2 * s + a)
 
-    def give(src, dst, device):
-        return remote(total.at[src], back.at[dst], back_send.at[src], back_recv.at[dst], device)
-
-    gives = (
-        [give(2, 0, ring(partner)), give(3, 1, ring(partner)), give(4, 2, ring(me + 2)), give(5, 3, ring(me + 2))],
-        [give(4, 2, ring(me + 2)), give(5, 3, ring(me + 2)), give(6, 4, ring(me - 2)), give(7, 5, ring(me - 2))],
-        [give(2, 0, ring(partner)), give(3, 1, ring(partner)), give(4, 2, ring(me - 2)), give(5, 4, ring(me + 2))],
-        [give(2, 0, ring(partner)), give(3, 1, ring(partner)), give(4, 3, ring(me - 3)), give(5, 5, ring(me + 1))],
-    )
+    @pl.when(role != 1)
+    def _():
+        for a in range(2):
+            give(2 + a, a, ring(partner)).start()
+
     takes = ([2, 3, 4, 5], [0, 1], [0, 1, 2, 3], [0, 1, 2, 3, 4, 5])
     for r in range(4):
         @pl.when(role == r)
         def _():
-            for copy in gives[r]:
-                copy.start()
-            for copy in gives[r]:
-                copy.wait_send()
             for b in takes[r]:
                 give(0, b, ring(partner)).wait_recv()
             for a in range(2):
@@ -342,27 +437,65 @@
                     if b % 2 == a:
                         whole = whole + back[b]
                 out_ref[a : a + 1] = jnp.where(bias[a] == 0.0, whole, 0.0)
+            for copy in gives[r]:
+                copy.wait_send()
+
+    @pl.when(role != 1)
+    def _():
+        for a in range(2):
+            give(2 + a, a, ring(partner)).wait_send()
+
+    spread(0, 1, ring(partner)).wait_send()
+
+    @pl.when(role != 1)
+    def _():
+        spread(1, 2, ring(partner)).wait_send()
+
+    @pl.when(role == 0)
+    def _():
+        spread(2, 2, ring(partner)).wait_send()
 
     @pl.when(role != 0)
     def _():
+        further().wait_send()
+
+    @pl.when(role != 0)
+    def _():
         near.wait_send()
 
-    @pl.when(role != 1)
-    def _():
-        for a, k in order:
-            own_piece(a, k, a, ring(partner)).wait_send()
+    def sent(a, pieces):
+        for k in pieces:
+            piece(x_hbm, a, k, a, ring(partner)).wait_send()
+
+    @pl.when(role == 0)
+    def _():
+        sent(0, range(chunks))
+        sent(1, range(chunks))
+
+    @pl.when(role == 2)
+    def _():
+        sent(1, range(chunks))
+        sent(0, direct[0])
+        for a, k in routed:
+            around(a, k).wait_send()
+
+    @pl.when(role == 3)
+    def _():
+        sent(0, range(chunks))
+        sent(1, direct[1])
 
     @pl.when(role == 1)
     def _():
-        for a, k in order:
-            passing(a, k).wait_send()
+        for k in range(chunks):
+            for a in range(2):
+                passing(a, k).wait_send()
 
     @pl.when(odd)
     def _():
         for k in range(chunks):
             passing(0, k).wait_send()
 
-    @pl.when(role == 2)
+    @pl.when(role == 3)
     def _():
         for a, k in routed:
             bypass(a, k).wait_send()
@@ -392,15 +525,16 @@
                 pltpu.VMEM((2, ROWS, width), jnp.bfloat16),
                 pltpu.VMEM((ROWS, length), jnp.float32),
                 pltpu.VMEM((ROWS, length), jnp.float32),
-                pltpu.VMEM((1 + len(LENS), answers, 128), jnp.int32),
+                pltpu.VMEM((4, answers, 128), jnp.int32),
                 pltpu.VMEM((4, 1, length), jnp.float32),
                 pltpu.VMEM((9, 1, length), jnp.float32),
                 pltpu.VMEM((9, 1, length), jnp.float32),
                 pltpu.VMEM((8, 1, length), jnp.float32),
                 pltpu.VMEM((6, 1, length), jnp.float32),
-                dma, dma((2,)), dma((len(LENS),)), dma((len(LENS),)),
-                dma((2, chunks)), dma((4, chunks)), dma((2, chunks)),
+                dma, dma((2,)), dma((4,)), dma((4,)),
+                dma((2, chunks)), dma((4, chunks)), dma((2, chunks)), dma((2, chunks)),
                 dma((2, chunks)), dma((2, chunks)), dma((8,)), dma((6,)),
+                pltpu.SemaphoreType.REGULAR, pltpu.SemaphoreType.REGULAR,
             ],
             compiler_params=pltpu.CompilerParams(collective_id=0, has_side_effects=True),
             name="consensus",

time: 77.2 us -> 70.7 us (0.916)
  the two profiles are of different devices: /device:TPU:2 before, /device:TPU:0 now
where the time goes in v2:
time: 70.7 us; the launch traced here: 70.5 us
  Pallas kernels  69.1 us (98%)
  other arithmetic  1.3 us (2%)
    pallas_call x1, Pallas kernels, shards(): pl.pallas_call(functools.partial(kernel, n, detour), out_shape=jax.ShapeD...  69.1 us

profile of v2, /device:TPU:0, one launch (start us, length us, event | category | flops | bytes accessed | tf_op | source)
XLA Modules:
  0.0 70.5 jit_solution(14065204084472437333)
XLA Ops:
  0.0 69.1 %consensus.1 = f32[2,1024]{1,0:T(2,128)} custom-call(bf16[2,1024,768]{2,1,0:T(8,128)(2,1)} %x_hbm.1, s32[2]{0:T(128)} %lens_ref.1), custom_call_target="tpu_custom_call" | custom-call | tf_op jit(solution)/shard_map/consensus/pallas_call | solution.py:512
  69.2 1.3 %broadcast_multiply_fusion = f32[2,1024]{1,0:T(2,128)} fusion(f32[2,1024]{1,0:T(2,128)} %consensus.1), kind=kLoop, calls=%fused_computation | loop fusion | flops 2048 | bytes 16384 | tf_op jit(solution)/shard_map/mul | solution.py:542

commit v3 on v2

--- a/solution.py
+++ b/solution.py
@@ -14,8 +14,8 @@
 PIECE = 128
 ROWS = 256
 WIDE = 256
-DETOUR = (3, 3)
-PACE = (0, 2, 2, 2, 0, 0, 0, 0)
+DETOUR = (3, 2)
+PACE = (0, 2, 2, 1, 0, 0, 0, 0)
 TURN = 1
 
 
@@ -397,7 +397,7 @@
 
         return carry
 
-    lax.fori_loop(0, 2 * chunks, step, 0)
+    lax.fori_loop(0, lag + chunks, step, 0)
 
     def give(src, dst, device):
         return remote(total.at[src], back.at[dst], back_send.at[src], back_recv.at[dst], device)

time: 70.7 us -> 69.6 us (0.984)
  Pallas kernels: 69.1 us -> 68.1 us
    pallas_call x1, Pallas kernels: 69.1 us -> 68.1 us  [shards(): pl.pallas_call(functools.partial(kernel, n, detour), out_shape=jax.ShapeD...]
where the time goes in v3:
time: 69.6 us; the launch traced here: 69.4 us
  Pallas kernels  68.1 us (98%)
  other arithmetic  1.3 us (2%)
    pallas_call x1, Pallas kernels, shards(): pl.pallas_call(functools.partial(kernel, n, detour), out_shape=jax.ShapeD...  68.1 us

profile of v3, /device:TPU:0, one launch (start us, length us, event | category | flops | bytes accessed | tf_op | source)
XLA Modules:
  0.0 69.4 jit_solution(14375284043180760807)
XLA Ops:
  0.0 68.1 %consensus.1 = f32[2,1024]{1,0:T(2,128)} custom-call(bf16[2,1024,768]{2,1,0:T(8,128)(2,1)} %x_hbm.1, s32[2]{0:T(128)} %lens_ref.1), custom_call_target="tpu_custom_call" | custom-call | tf_op jit(solution)/shard_map/consensus/pallas_call | solution.py:512
  68.1 1.3 %broadcast_multiply_fusion = f32[2,1024]{1,0:T(2,128)} fusion(f32[2,1024]{1,0:T(2,128)} %consensus.1), kind=kLoop, calls=%fused_computation | loop fusion | flops 2048 | bytes 16384 | tf_op jit(solution)/shard_map/mul | solution.py:542

commit v4 on v3

--- a/solution.py
+++ b/solution.py
@@ -326,6 +326,13 @@
     lag = jnp.where(role == 0, chunks, per)
 
     def step(j, carry):
+        @pl.when(j == chunks)
+        def _():
+            close(0, 8)
+            for s in range(2):
+                for a in range(2):
+                    close(base + a, 2 * s + a)
+
         @pl.when(role == 2)
         def _():
             routes(j, lambda a, k: around(a, k).start())
@@ -414,8 +421,7 @@
             for copy in gives[r]:
                 copy.start()
 
-    close(0, 8)
-    for s in range(4):
+    for s in range(2, 4):
         left = last if s == 3 else base
         for a in range(2):
             close(left + a, 2 * s + a)

time: 69.6 us -> 69.6 us (level)
  no operation moved by 1% of the time
where the time goes in v4:
time: 69.6 us; the launch traced here: 69.4 us
  Pallas kernels  68.1 us (98%)
  other arithmetic  1.3 us (2%)
    pallas_call x1, Pallas kernels, shards(): pl.pallas_call(functools.partial(kernel, n, detour), out_shape=jax.ShapeD...  68.1 us

profile of v4, /device:TPU:0, one launch (start us, length us, event | category | flops | bytes accessed | tf_op | source)
XLA Modules:
  0.0 69.4 jit_solution(7658231686069850752)
XLA Ops:
  0.0 68.1 %consensus.1 = f32[2,1024]{1,0:T(2,128)} custom-call(bf16[2,1024,768]{2,1,0:T(8,128)(2,1)} %x_hbm.1, s32[2]{0:T(128)} %lens_ref.1), custom_call_target="tpu_custom_call" | custom-call | tf_op jit(solution)/shard_map/consensus/pallas_call | solution.py:518
  68.1 1.3 %broadcast_multiply_fusion = f32[2,1024]{1,0:T(2,128)} fusion(f32[2,1024]{1,0:T(2,128)} %consensus.1), kind=kLoop, calls=%fused_computation | loop fusion | flops 2048 | bytes 16384 | tf_op jit(solution)/shard_map/mul | solution.py:548

commit v5 on v4

--- a/solution.py
+++ b/solution.py
@@ -323,6 +323,16 @@
         around(a, k).wait_recv()
         bypass(a, k).start()
 
+    def give(src, dst, device):
+        return remote(total.at[src], back.at[dst], back_send.at[src], back_recv.at[dst], device)
+
+    early = (
+        [],
+        [give(4, 2, ring(me + 2)), give(5, 3, ring(me + 2))],
+        [give(4, 2, ring(me - 2))],
+        [give(4, 3, ring(me - 3))],
+    )
+
     lag = jnp.where(role == 0, chunks, per)
 
     def step(j, carry):
@@ -332,6 +342,11 @@
             for s in range(2):
                 for a in range(2):
                     close(base + a, 2 * s + a)
+            for r in range(1, 4):
+                @pl.when(role == r)
+                def _():
+                    for copy in early[r]:
+                        copy.start()
 
         @pl.when(role == 2)
         def _():
@@ -406,14 +421,11 @@
 
     lax.fori_loop(0, lag + chunks, step, 0)
 
-    def give(src, dst, device):
-        return remote(total.at[src], back.at[dst], back_send.at[src], back_recv.at[dst], device)
-
     gives = (
         [give(4, 2, ring(me + 2)), give(5, 3, ring(me + 2))],
-        [give(6, 4, ring(me - 2)), give(7, 5, ring(me - 2)), give(4, 2, ring(me + 2)), give(5, 3, ring(me + 2))],
-        [give(5, 4, ring(me + 2)), give(4, 2, ring(me - 2))],
-        [give(5, 5, ring(me + 1)), give(4, 3, ring(me - 3))],
+        [give(6, 4, ring(me - 2)), give(7, 5, ring(me - 2))],
+        [give(5, 4, ring(me + 2))],
+        [give(5, 5, ring(me + 1))],
     )
     for r in range(4):
         @pl.when(role == r)
@@ -443,7 +455,7 @@
                     if b % 2 == a:
                         whole = whole + back[b]
                 out_ref[a : a + 1] = jnp.where(bias[a] == 0.0, whole, 0.0)
-            for copy in gives[r]:
+            for copy in gives[r] + early[r]:
                 copy.wait_send()
 
     @pl.when(role != 1)

time: 69.6 us -> 69.6 us (level)
  no operation moved by 1% of the time
where the time goes in v5:
time: 69.6 us; the launch traced here: 69.4 us
  Pallas kernels  68.1 us (98%)
  other arithmetic  1.3 us (2%)
    pallas_call x1, Pallas kernels, shards(): pl.pallas_call(functools.partial(kernel, n, detour), out_shape=jax.ShapeD...  68.1 us

profile of v5, /device:TPU:0, one launch (start us, length us, event | category | flops | bytes accessed | tf_op | source)
XLA Modules:
  0.0 69.4 jit_solution(9702399679084493771)
XLA Ops:
  0.0 68.1 %consensus.1 = f32[2,1024]{1,0:T(2,128)} custom-call(bf16[2,1024,768]{2,1,0:T(8,128)(2,1)} %x_hbm.1, s32[2]{0:T(128)} %lens_ref.1), custom_call_target="tpu_custom_call" | custom-call | tf_op jit(solution)/shard_map/consensus/pallas_call | solution.py:530
  68.1 1.3 %broadcast_multiply_fusion = f32[2,1024]{1,0:T(2,128)} fusion(f32[2,1024]{1,0:T(2,128)} %consensus.1), kind=kLoop, calls=%fused_computation | loop fusion | flops 2048 | bytes 16384 | tf_op jit(solution)/shard_map/mul | solution.py:560

commit v6 on v4

--- a/solution.py
+++ b/solution.py
@@ -14,8 +14,8 @@
 PIECE = 128
 ROWS = 256
 WIDE = 256
-DETOUR = (3, 2)
-PACE = (0, 2, 2, 1, 0, 0, 0, 0)
+DETOUR = (3, 3)
+PACE = (0, 2, 2, 2, 0, 0, 0, 0)
 TURN = 1
 
 

time: 69.6 us -> 69.9 us (level)
  no operation moved by 1% of the time
where the time goes in v6:
time: 69.9 us; the launch traced here: 69.7 us
  Pallas kernels  68.4 us (98%)
  other arithmetic  1.3 us (2%)
    pallas_call x1, Pallas kernels, shards(): pl.pallas_call(functools.partial(kernel, n, detour), out_shape=jax.ShapeD...  68.4 us

profile of v6, /device:TPU:0, one launch (start us, length us, event | category | flops | bytes accessed | tf_op | source)
XLA Modules:
  0.0 69.7 jit_solution(12306949558260683732)
XLA Ops:
  0.0 68.4 %consensus.1 = f32[2,1024]{1,0:T(2,128)} custom-call(bf16[2,1024,768]{2,1,0:T(8,128)(2,1)} %x_hbm.1, s32[2]{0:T(128)} %lens_ref.1), custom_call_target="tpu_custom_call" | custom-call | tf_op jit(solution)/shard_map/consensus/pallas_call | solution.py:518
  68.4 1.3 %broadcast_multiply_fusion = f32[2,1024]{1,0:T(2,128)} fusion(f32[2,1024]{1,0:T(2,128)} %consensus.1), kind=kLoop, calls=%fused_computation | loop fusion | flops 2048 | bytes 16384 | tf_op jit(solution)/shard_map/mul | solution.py:548
